TPU v7x, 32 devices: a whole 2x2x4 slice. The times are simulated.
32 devices in a mesh: grp: 2 (over y), gene: 4 (over z), cell: 4 (over x, core).
Axes of the slice: x: 2, y: 2, z: 4, core: 2. Of those that a mesh axis runs over, the one named last changes fastest.
Arguments:
- expression: bfloat16 [4096, 32768], P(('grp', 'cell'), 'gene'), parts along dimension 0, may hold values from -6 to 6
- gene_mask: int32 [4096, 32768], P(('grp', 'cell'), 'gene'), parts along dimension 0, may hold values 0 or 1
- mask_value: bfloat16 [32768], P('gene'), may hold values from -4 to 4
- w_qkv: bfloat16 [32768, 3072], P('gene'), may hold values from -0.03125 to 0.03125
- w_out: bfloat16 [1024, 32768], P(None, 'gene'), may hold values from -1.5 to 1.5
- w_first: bfloat16 [128, 256, 256], P('gene'), may hold values from -0.375 to 0.375
- w_second: bfloat16 [128, 256, 256], P('gene'), may hold values from -0.375 to 0.375
- cotangent: bfloat16 [4096, 32768], P(('grp', 'cell'), 'gene'), parts along dimension 0, may hold values from -6 to 6
Outputs:
- denoised: bfloat16 [4096, 32768], P(('grp', 'cell'), 'gene'), parts along dimension 0
- grad_first: float32 [256, 256, 256], P(('grp', 'gene'), 'cell'), parts along dimension 0
- grad_second: float32 [256, 256, 256], P(('grp', 'gene'), 'cell'), parts along dimension 0
There are 2 independent parts, one for each index of `grp`. A program takes and returns all parts, laid end to end along the dimension named above; an argument that names none is the same for every part. Nothing has to cross between parts.
All inputs are finite; a program needn't handle non-finite values. No bound on the sum of `gene_mask` on one device may be relied on, other than what follows from the above.
Results may differ from a plain program's by a relative error of at most 0.02.
Values may be sent and summed in bfloat16 or wider, within the bound.
A program may use at most 256 MiB of HBM per device.

v0:
```python
import jax
import jax.numpy as jnp
from jax import lax
from jax.sharding import PartitionSpec as P

HEADS = 16
HEAD_DIM = 64


def normalize(part):
    count = part.shape[0]
    shaped = part.reshape(count, HEADS, HEAD_DIM)
    meansq = jnp.mean(shaped * shaped, axis=-1, keepdims=True)
    return (
        (shaped * lax.rsqrt(meansq + 1e-06)).astype(jnp.bfloat16).reshape(count, HEADS * HEAD_DIM)
    )


def split_heads(qkv_sums):
    columns = qkv_sums.shape[1] // 3
    queries = normalize(qkv_sums[:, :columns])
    keys_normed = normalize(qkv_sums[:, columns : 2 * columns])
    values_b = qkv_sums[:, 2 * columns :].astype(jnp.bfloat16)
    return (queries, keys_normed, values_b)


def attend(queries, pieces):
    key_piece, value_piece = pieces
    query_count = queries.shape[0]
    key_count = key_piece.shape[0]
    query_heads = queries.reshape(query_count, HEADS, HEAD_DIM)
    key_heads = key_piece.reshape(key_count, HEADS, HEAD_DIM)
    value_heads = value_piece.reshape(key_count, HEADS, HEAD_DIM)
    scores = jnp.einsum(
        "qhd,khd->hqk", query_heads, key_heads, preferred_element_type=jnp.float32
    ) * HEAD_DIM ** (-0.5)
    expw = jnp.exp(scores).astype(jnp.bfloat16)
    denom = jnp.sum(expw, axis=2, dtype=jnp.float32)
    numer = jnp.einsum("hqk,khd->qhd", expw, value_heads, preferred_element_type=jnp.float32)
    return (numer, denom)


def finish(totals):
    numer, denom = totals
    query_count = numer.shape[0]
    return (numer / denom.T[:, :, None]).astype(jnp.bfloat16).reshape(query_count, HEADS * HEAD_DIM)


def on_device(expression, gene_mask, mask_value, w_qkv, w_out, w_first, w_second, cotangent):
    groups = lax.axis_size("gene")
    local_blocks = w_first.shape[0]
    block_size = w_first.shape[1]
    block_total = local_blocks * groups
    cell_rows = expression.shape[0]
    masked_in = jnp.where(gene_mask == 1, mask_value[None, :], expression)
    qkv_part = jnp.dot(masked_in, w_qkv, preferred_element_type=jnp.float32)
    qkv_full = lax.psum(qkv_part.astype(jnp.bfloat16), "gene").astype(jnp.float32)
    queries, keys_normed, values_b = split_heads(qkv_full)
    totals = attend(
        queries,
        (
            lax.all_gather(keys_normed, "cell", axis=0, tiled=True),
            lax.all_gather(values_b, "cell", axis=0, tiled=True),
        ),
    )
    attended = finish(totals)
    added = jnp.dot(attended, w_out, preferred_element_type=jnp.float32)
    hidden = (masked_in.astype(jnp.float32) + added).astype(jnp.bfloat16)
    blocks = hidden.reshape(cell_rows, local_blocks, block_size)
    first = jnp.einsum("cbi,bio->cbo", blocks, w_first, preferred_element_type=jnp.float32).astype(
        jnp.bfloat16
    )
    cot_blocks = cotangent.reshape(cell_rows, local_blocks, block_size)
    back_perm = jnp.einsum(
        "cjo,jko->cjk", cot_blocks, w_second, preferred_element_type=jnp.float32
    ).astype(jnp.bfloat16)
    back_send = back_perm.reshape(cell_rows, block_size // groups, block_total)
    received = lax.all_to_all(first, "gene", split_axis=2, concat_axis=1, tiled=True)
    permuted = jnp.swapaxes(received, 1, 2).reshape(cell_rows, local_blocks, block_size)
    mixed = jnp.einsum("cjk,jko->cjo", permuted, w_second, preferred_element_type=jnp.float32)
    denoised = (
        (blocks.astype(jnp.float32) + mixed)
        .astype(jnp.bfloat16)
        .reshape(cell_rows, local_blocks * block_size)
    )
    grad_second = jnp.einsum(
        "cjk,cjo->jko", permuted, cot_blocks, preferred_element_type=jnp.float32
    )
    back_recv = lax.all_to_all(back_send, "gene", split_axis=2, concat_axis=1, tiled=True)
    back_first = jnp.swapaxes(back_recv, 1, 2)
    grad_first = jnp.einsum("cbi,cbo->bio", blocks, back_first, preferred_element_type=jnp.float32)
    first_share, second_share = (
        lax.psum_scatter(
            grad_first.astype(jnp.bfloat16), "cell", scatter_dimension=1, tiled=True
        ).astype(jnp.float32),
        lax.psum_scatter(
            grad_second.astype(jnp.bfloat16), "cell", scatter_dimension=1, tiled=True
        ).astype(jnp.float32),
    )
    return (denoised, first_share, second_share)


def solution(mesh):
    placed = (
        P(("grp", "cell"), "gene"),
        P(("grp", "cell"), "gene"),
        P("gene"),
        P("gene", None),
        P(None, "gene"),
        P("gene", None, None),
        P("gene", None, None),
        P(("grp", "cell"), "gene"),
    )
    return jax.shard_map(
        on_device,
        mesh=mesh,
        in_specs=placed,
        out_specs=(
            P(("grp", "cell"), "gene"),
            P(("grp", "gene"), "cell", None),
            P(("grp", "gene"), "cell", None),
        ),
        check_vma=False,
    )
```

profile of v0, /device:TPU:0, one launch (start us, length us, event | category | flops | bytes accessed | tf_op | source)
XLA Modules:
  0.0 680.9 jit_solution(10328082861231233537)
XLA Ops:
  7.2 9.0 %compare_select_fusion = bf16[512,8192]{1,0:T(8,128)(2,1)S(1)} fusion(bf16[512,8192]{1,0:T(8,128)(2,1)} %param.8, s32[512,8192]{1,0:T(8,128)} %param.9, bf16[8192]{0:T(1024)(128)(2,1)} %param.10), kind=kLoop, calls=%fused_computation.5 | loop fusion | flops 8388608 | bytes 33570816 | tf_op jit(solution)/shard_map/jit(_where)/select_n | solution.py:55
  19.7 32.1 %convolution_convert_fusion = bf16[512,3072]{1,0:T(8,128)(2,1)} fusion(bf16[512,8192]{1,0:T(8,128)(2,1)S(1)} %compare_select_fusion, bf16[8192,3072]{1,0:T(8,128)(2,1)} %param.11), kind=kOutput, calls=%fused_computation.16 | convolution fusion | flops 25771376640 | bytes 61865984 | tf_op jit(solution)/shard_map/dot_general | solution.py:56
  51.9 123.9 %all-reduce.2.cloned.1.call-done = bf16[512,3072]{1,0:T(8,128)(2,1)} async-done(((bf16[512,3072]{1,0:T(8,128)(2,1)}), bf16[512,3072]{1,0:T(8,128)(2,1)}) %all-reduce.2.cloned.1.call-update) | async-done | bytes 3145744 | tf_op jit(solution)/shard_map/psum | solution.py:57
  194.8 10.7 %fusion.9 = bf16[32,256,512]{2,1,0:T(8,128)(2,1)} fusion(bf16[32,256,256]{2,1,0:T(8,128)(2,1)} %param.14, bf16[64,32,8,256]{3,2,1,0:T(8,128)(2,1)} %bitcast.75), kind=kOutput, calls=%fused_computation.15 | convolution fusion | flops 2151677952 | bytes 20971520 | tf_op jit(solution)/shard_map/cjo,jko->cjk/dot_general | solution.py:74
  205.5 11.4 %copy.73 = bf16[512,64,128]{0,1,2:T(8,128)(2,1)} copy(bf16[512,64,128]{0,2,1:T(8,128)(2,1)} %bitcast.72) | data formatting | bytes 16777216 | tf_op jit(solution)/shard_map/reshape | solution.py:77
  226.8 6.5 copy.63
  233.3 30.1 %all-gather.3.cloned.1.call-done = bf16[2048,1024]{1,0:T(8,128)(2,1)} async-done(((bf16[512,1024]{1,0:T(8,128)(2,1)}), bf16[2048,1024]{1,0:T(8,128)(2,1)}) %all-gather.3.cloned.1.call-update) | async-done | bytes 4194320 | tf_op jit(solution)/shard_map/all_gather | solution.py:63
  269.9 18.0 %convert_reduce_fusion = (f32[16,512]{1,0:T(8,128)S(1)}, bf16[16,512,2048]{2,1,0:T(8,128)(2,1)}) fusion(bf16[2048,16,64]{0,2,1:T(8,128)(2,1)} %bitcast.79, f32[512,16,64]{0,2,1:T(8,128)S(1)} %bitcast.77, f32[512,16]{0,1:T(8,128)S(1)} %add_rsqrt_fusion.1), kind=kOutput, calls=%fused_computation | convolution fusion | flops 2215632896 | bytes 39911424 | tf_op jit(solution)/shard_map/qhd,khd->hqk/dot_general | solution.py:34
  287.9 17.0 %fusion.18 = bf16[512,16,64]{0,2,1:T(8,128)(2,1)S(1)} fusion(bf16[2048,16,64]{0,2,1:T(8,128)(2,1)} %bitcast.73, bf16[16,512,2048]{2,1,0:T(8,128)(2,1)} %get-tuple-element.16, f32[512,16]{0,1:T(8,128)S(1)} %bitcast.80), kind=kOutput, calls=%fused_computation.20 | convolution fusion | flops 2148532224 | bytes 38830080 | tf_op jit(solution)/shard_map/hqk,khd->qhd/dot_general | solution.py:39
  304.9 18.4 %add_convert_fusion = bf16[512,8192]{1,0:T(8,128)(2,1)} fusion(bf16[512,8192]{1,0:T(8,128)(2,1)} %copy-done, bf16[512,1024]{0,1:T(8,128)(2,1)S(1)} %bitcast.74, bf16[1024,8192]{1,0:T(8,128)(2,1)} %param.12), kind=kOutput, calls=%fused_computation.4 | convolution fusion | flops 8602517504 | bytes 34603008 | tf_op jit(solution)/shard_map/dot_general | solution.py:67
  323.3 12.0 %copy.84 = bf16[512,8192]{0,1:T(8,128)(2,1)} copy(bf16[512,8192]{1,0:T(8,128)(2,1)} %add_convert_fusion) | data formatting | bytes 16777216 | tf_op jit(solution)/shard_map/reshape | solution.py:69
  335.3 8.4 %convert_bitcast_fusion = bf16[512,32,256]{2,0,1:T(8,128)(2,1)} fusion(bf16[512,32,256]{0,2,1:T(8,128)(2,1)} %bitcast.64, bf16[32,256,256]{2,1,0:T(8,128)(2,1)} %param.13), kind=kOutput, calls=%fused_computation.12 | convolution fusion | flops 2151677952 | bytes 20971520 | tf_op jit(solution)/shard_map/cbi,bio->cbo/dot_general | solution.py:70
  343.7 14.7 %copy.66 = bf16[512,32,256]{0,1,2:T(8,128)(2,1)} copy(bf16[512,32,256]{2,0,1:T(8,128)(2,1)} %convert_bitcast_fusion) | data formatting | bytes 16777216 | tf_op jit(solution)/shard_map/convert_element_type | solution.py:70
  358.4 47.4 %all-to-all-done.1 = bf16[512,64,128]{0,1,2:T(8,128)(2,1)} async-done(((bf16[512,64,128]{0,1,2:T(8,128)(2,1)}), bf16[512,64,128]{0,1,2:T(8,128)(2,1)}, u32[]{:S(2)}, u32[]{:S(2)}) %all-to-all-start.1) | async-done | bytes 8388640 | tf_op jit(solution)/shard_map/all_to_all | solution.py:89
  411.5 11.6 %copy.75 = bf16[512,4,64,32]{0,3,2,1:T(8,128)(2,1)} copy(bf16[512,4,64,32]{0,2,3,1:T(8,128)(2,1)} %bitcast.21) | data formatting | bytes 16777216 | tf_op jit(solution)/shard_map/all_to_all | solution.py:89
  423.1 13.7 %copy.76 = bf16[512,256,32]{1,0,2:T(8,128)(2,1)} copy(bf16[512,256,32]{0,2,1:T(8,128)(2,1)} %bitcast.70) | data formatting | bytes 16777216 | tf_op jit(solution)/shard_map/all_to_all | solution.py:89
  436.8 10.2 %fusion.12 = bf16[32,256,256]{2,1,0:T(8,128)(2,1)} fusion(bf16[512,32,256]{0,2,1:T(8,128)(2,1)} %bitcast.65, bf16[512,256,32]{1,0,2:T(8,128)(2,1)} %copy.76), kind=kOutput, calls=%fused_computation.17 | convolution fusion | flops 2149580800 | bytes 20971520 | tf_op jit(solution)/shard_map/cbi,cbo->bio/dot_general | solution.py:91
  447.3 146.7 %all-to-all-done = bf16[512,32,256]{0,1,2:T(8,128)(2,1)} async-done(((bf16[512,32,256]{0,1,2:T(8,128)(2,1)}), bf16[512,32,256]{0,1,2:T(8,128)(2,1)}, u32[]{:S(2)}, u32[]{:S(2)}) %all-to-all-start) | async-done | bytes 8388640 | tf_op jit(solution)/shard_map/all_to_all | solution.py:78
  594.1 11.6 %copy.68 = bf16[512,4,32,64]{0,3,2,1:T(8,128)(2,1)} copy(bf16[512,4,32,64]{0,2,3,1:T(8,128)(2,1)} %bitcast.11) | data formatting | bytes 16777216 | tf_op jit(solution)/shard_map/all_to_all | solution.py:78
  605.7 11.3 %copy.69 = bf16[512,64,128]{0,2,1:T(8,128)(2,1)} copy(bf16[512,64,128]{0,1,2:T(8,128)(2,1)} %bitcast.71) | data formatting | bytes 16777216 | tf_op jit(solution)/shard_map/transpose | solution.py:79
  617.0 10.4 %fusion.15 = bf16[32,256,256]{2,1,0:T(8,128)(2,1)} fusion(bf16[512,32,256]{0,2,1:T(8,128)(2,1)} %bitcast.67, bf16[64,32,8,256]{3,2,1,0:T(8,128)(2,1)} %bitcast.76), kind=kOutput, calls=%fused_computation.18 | convolution fusion | flops 2149580800 | bytes 20971520 | tf_op jit(solution)/shard_map/cjk,cjo->jko/dot_general | solution.py:86
  630.2 12.9 %fusion = bf16[512,32,256]{0,2,1:T(8,128)(2,1)} fusion(bf16[512,32,256]{0,2,1:T(8,128)(2,1)} %bitcast.66, bf16[512,32,256]{0,2,1:T(8,128)(2,1)} %bitcast.68, bf16[32,256,256]{2,1,0:T(8,128)(2,1)} %param.14), kind=kOutput, calls=%fused_computation.3 | convolution fusion | flops 2160066560 | bytes 29360128 | tf_op jit(solution)/shard_map/cjk,jko->cjo/dot_general | solution.py:80
  643.1 12.0 %copy.79 = bf16[512,8192]{1,0:T(8,128)(2,1)} copy(bf16[512,8192]{0,1:T(8,128)(2,1)} %bitcast.69) | data formatting | bytes 16777216
  655.1 15.9 %reduce-scatter.5.cloned.1.call-done = bf16[32,64,256]{2,1,0:T(8,128)(2,1)} async-done(((bf16[32,256,256]{2,1,0:T(8,128)(2,1)}), bf16[32,64,256]{2,1,0:T(8,128)(2,1)}) %reduce-scatter.5.cloned.1.call-update) | async-done | bytes 1048592 | tf_op jit(solution)/shard_map/reduce_scatter | solution.py:96
  (36 shorter events, 50.5 us)
Async XLA Ops:
  7.2 168.6 %all-reduce.2.cloned.1.call-start = ((), (), s32[]{:S(2)}) async-start(), calls=%async_computation.4 | async-start | bytes 6291456 | tf_op jit(solution)/shard_map/psum | solution.py:57
  16.3 3.4 copy-start
  51.8 175.0 %all-gather.5.cloned.1.call-start = ((), (), s32[]{:S(2)}) async-start(), calls=%async_computation.6 | async-start | bytes 5242880 | tf_op jit(solution)/shard_map/all_gather | solution.py:62
  178.4 2.7 copy-start.1
  183.1 10.6 %copy-start.2 = (bf16[512,3072]{1,0:T(8,128)(2,1)S(1)}, bf16[512,3072]{1,0:T(8,128)(2,1)}, u32[]{:S(2)}) copy-start(bf16[512,3072]{1,0:T(8,128)(2,1)} %all-reduce.2.cloned.1.call-done) | copy-start | bytes 9437188
  193.1 70.3 %all-gather.3.cloned.1.call-start = ((), (), s32[]{:S(2)}) async-start(), calls=%async_computation.5 | async-start | bytes 5242880 | tf_op jit(solution)/shard_map/all_gather | solution.py:63
  216.8 189.0 %all-to-all-start.1 = ((bf16[512,64,128]{0,1,2:T(8,128)(2,1)}), bf16[512,64,128]{0,1,2:T(8,128)(2,1)}, u32[]{:S(2)}, u32[]{:S(2)}) async-start(bf16[512,64,128]{0,1,2:T(8,128)(2,1)} %copy.73), calls=%async_computation.1 | async-start | bytes 16777216 | tf_op jit(solution)/shard_map/all_to_all | solution.py:89
  405.8 188.3 %all-to-all-start = ((bf16[512,32,256]{0,1,2:T(8,128)(2,1)}), bf16[512,32,256]{0,1,2:T(8,128)(2,1)}, u32[]{:S(2)}, u32[]{:S(2)}) async-start(bf16[512,32,256]{0,1,2:T(8,128)(2,1)} %copy.66), calls=%async_computation | async-start | bytes 16777216 | tf_op jit(solution)/shard_map/all_to_all | solution.py:78
  411.5 216.0 %reduce-scatter.3.cloned.1.call-start = ((), (), s32[]{:S(2)}) async-start(), calls=%async_computation.7 | async-start | bytes 5242880 | tf_op jit(solution)/shard_map/reduce_scatter | solution.py:93
  447.0 224.0 %reduce-scatter.5.cloned.1.call-start = ((), (), s32[]{:S(2)}) async-start(), calls=%async_computation.8 | async-start | bytes 5242880 | tf_op jit(solution)/shard_map/reduce_scatter | solution.py:96
Sparse Core Ops, SparseCore 0:
  51.9 123.7 all-reduce.1
  193.3 33.4 all-gather.4
  228.9 34.4 all-gather.2
  447.2 45.6 reduce-scatter.2
  627.5 43.4 reduce-scatter.4
where the time goes:
time: 688 us; the launch traced here: 681 us
  waiting for transfers between devices  364 us (53%)
  matrix products  138 us (20%)
  local copies, waits for them, and re-layouts  128 us (19%)
  other arithmetic  23.4 us (3%)
  between operations  14.4 us (2%)
  starting transfers between devices  12.4 us (2%)
    all_to_all x1, waiting for transfers between devices, on_device(): lax.all_to_all(first, 'gene', split_axis=2, concat_axis=1, tiled=True)  147 us
    psum x1, waiting for transfers between devices, on_device(): lax.psum(qkv_part.astype(jnp.bfloat16), 'gene').astype(jnp.float32)  124 us
    all_to_all x1, waiting for transfers between devices, on_device(): lax.all_to_all(back_send, 'gene', split_axis=2, concat_axis=1, tiled=True)  47.4 us
    dot_general x1, matrix products, on_device(): qkv_part = jnp.dot(masked_in, w_qkv, preferred_element_type=jnp.float32)  32.1 us
    all_gather x1, waiting for transfers between devices, on_device(): lax.all_gather(values_b, 'cell', axis=0, tiled=True)  30.1 us
    all_to_all x2, local copies, waits for them, and re-layouts, on_device(): lax.all_to_all(back_send, 'gene', split_axis=2, concat_axis=1, tiled=True)  25.3 us
    dot_general x1, matrix products, on_device(): added = jnp.dot(attended, w_out, preferred_element_type=jnp.float32)  18.4 us
    unnamed x7, local copies, waits for them, and re-layouts  18 us
  transfers between devices with their start and end apart: 7, of which 6 were waited for; matrix products, arithmetic and copies ran while one was open for 33% of the time, Pallas kernels for 0%

commit v1 on v0

v1 whole, which is shorter than its diff:
```python
import jax
import jax.numpy as jnp
from jax import lax
from jax.experimental import pallas as pl
from jax.sharding import PartitionSpec as P

HEADS = 16
HEAD_DIM = 64
BACK_CHUNKS = 4
FIRST_CHUNKS = 2


def normalize(part):
    count, columns = part.shape
    shaped = part.reshape(count, columns // HEAD_DIM, HEAD_DIM)
    meansq = jnp.mean(shaped * shaped, axis=-1, keepdims=True)
    return (shaped * lax.rsqrt(meansq + 1e-06)).astype(jnp.bfloat16).reshape(count, columns)


def attend(queries, key_piece, value_piece):
    query_count, columns = queries.shape
    key_count = key_piece.shape[0]
    heads = columns // HEAD_DIM
    query_heads = queries.reshape(query_count, heads, HEAD_DIM)
    key_heads = key_piece.reshape(key_count, heads, HEAD_DIM)
    value_heads = value_piece.reshape(key_count, heads, HEAD_DIM)
    scores = jnp.einsum(
        "qhd,khd->hqk", query_heads, key_heads, preferred_element_type=jnp.float32
    ) * HEAD_DIM ** (-0.5)
    expw = jnp.exp(scores).astype(jnp.bfloat16)
    denom = jnp.sum(expw, axis=2, dtype=jnp.float32)
    numer = jnp.einsum("hqk,khd->qhd", expw, value_heads, preferred_element_type=jnp.float32)
    return (numer / denom.T[:, :, None]).astype(jnp.bfloat16).reshape(query_count, columns)


def scattered_projection(masked_in, weight, groups, kinds):
    rows = masked_in.shape[0]
    part = jnp.dot(masked_in, weight, preferred_element_type=jnp.float32).astype(jnp.bfloat16)
    if HEADS % groups:
        return lax.psum(part, "gene").astype(jnp.float32).reshape(rows, kinds, -1)
    if kinds == 1:
        share = lax.psum_scatter(part, "gene", scatter_dimension=1, tiled=True)
        return share.astype(jnp.float32).reshape(rows, 1, -1)
    apart = part.reshape(rows, kinds, groups, -1).transpose(2, 1, 0, 3)
    share = lax.psum_scatter(apart, "gene", scatter_dimension=0, tiled=False)
    return share.transpose(1, 0, 2).astype(jnp.float32)


def cost(flops, moved):
    return pl.CostEstimate(flops=flops, bytes_accessed=moved, transcendentals=0)


def back_body(cot_ref, weight_ref, *out_refs):
    groups, _, pair, step, _ = out_refs[0].shape
    rows = lax.dot_general(
        weight_ref[0], cot_ref[...], (((1,), (1,)), ((), ())), preferred_element_type=jnp.float32
    )
    for index, out_ref in enumerate(out_refs):
        for g in range(groups):
            for r in range(pair):
                start = ((r * groups + g) * len(out_refs) + index) * step
                out_ref[g, 0, r] = rows[start : start + step].astype(out_ref.dtype)


def back_factor(cotangent, w_second, groups, pair, chunks):
    cells = cotangent.shape[0]
    local_blocks, block_size, _ = w_second.shape
    step = local_blocks // chunks
    return pl.pallas_call(
        back_body,
        grid=(local_blocks,),
        in_specs=[
            pl.BlockSpec((cells, block_size), lambda j: (0, j)),
            pl.BlockSpec((1, block_size, block_size), lambda j: (j, 0, 0)),
        ],
        out_specs=[
            pl.BlockSpec((groups, 1, pair, step, cells), lambda j: (0, j, 0, 0, 0))
        ]
        * chunks,
        out_shape=[
            jax.ShapeDtypeStruct((groups, local_blocks, pair, step, cells), jnp.bfloat16)
        ]
        * chunks,
        cost_estimate=cost(
            2 * cells * local_blocks * block_size**2, 5 * cells * local_blocks * block_size
        ),
    )(cotangent, w_second)


def first_body(attended_ref, out_weight_ref, masked_ref, weight_ref, hidden_ref, *first_refs):
    groups, _, step, _ = first_refs[0].shape
    added = jnp.dot(attended_ref[...], out_weight_ref[...], preferred_element_type=jnp.float32)
    hidden = (masked_ref[...].astype(jnp.float32) + added).astype(hidden_ref.dtype)
    hidden_ref[...] = hidden
    rows = lax.dot_general(
        weight_ref[0], hidden, (((0,), (1,)), ((), ())), preferred_element_type=jnp.float32
    )
    for index, first_ref in enumerate(first_refs):
        for g in range(groups):
            start = (g * len(first_refs) + index) * step
            first_ref[g, 0] = rows[start : start + step].astype(first_ref.dtype)


def first_factor(attended, w_out, masked_in, w_first, groups, chunks):
    cells, width = attended.shape
    local_blocks, block_size, _ = w_first.shape
    step = block_size // groups // chunks
    columns = pl.BlockSpec((cells, block_size), lambda b: (0, b))
    return pl.pallas_call(
        first_body,
        grid=(local_blocks,),
        in_specs=[
            pl.BlockSpec((cells, width), lambda b: (0, 0)),
            pl.BlockSpec((width, block_size), lambda b: (0, b)),
            columns,
            pl.BlockSpec((1, block_size, block_size), lambda b: (b, 0, 0)),
        ],
        out_specs=[columns]
        + [pl.BlockSpec((groups, 1, step, cells), lambda b: (0, b, 0, 0))] * chunks,
        out_shape=[jax.ShapeDtypeStruct(masked_in.shape, jnp.bfloat16)]
        + [jax.ShapeDtypeStruct((groups, local_blocks, step, cells), jnp.bfloat16)] * chunks,
        cost_estimate=cost(
            2 * cells * local_blocks * block_size * (block_size + width),
            2 * local_blocks * block_size * (3 * cells + width + block_size),
        ),
    )(attended, w_out, masked_in, w_first)


def grad_body(got_ref, hidden_ref, grad_ref):
    rows = jnp.dot(got_ref[0], hidden_ref[...], preferred_element_type=jnp.float32)
    grad_ref[0] = rows.T.astype(grad_ref.dtype)


def first_gradient(got, hidden, at, step):
    _, block_size, cells = got.shape
    return pl.pallas_call(
        grad_body,
        grid=(step,),
        in_specs=[
            pl.BlockSpec((1, block_size, cells), lambda b: (at + b, 0, 0)),
            pl.BlockSpec((cells, block_size), lambda b: (0, at + b)),
        ],
        out_specs=pl.BlockSpec((1, block_size, block_size), lambda b: (b, 0, 0)),
        out_shape=jax.ShapeDtypeStruct((step, block_size, block_size), jnp.bfloat16),
        cost_estimate=cost(2 * step * cells * block_size**2, 5 * step * cells * block_size),
    )(got, hidden)


def second_body(permuted_ref, cot_ref, hidden_ref, weight_ref, *rest):
    out_ref, grad_ref = rest[-2:]
    permuted = permuted_ref[0]
    mixed = lax.dot_general(
        permuted, weight_ref[0], (((0,), (0,)), ((), ())), preferred_element_type=jnp.float32
    )
    out_ref[...] = (hidden_ref[...].astype(jnp.float32) + mixed).astype(out_ref.dtype)
    grad_ref[0] = jnp.dot(
        permuted, cot_ref[...], preferred_element_type=jnp.float32
    ).astype(grad_ref.dtype)


def second_factor(permuted, cotangent, hidden, w_second, at, denoised):
    step, block_size, cells = permuted.shape
    columns = pl.BlockSpec((cells, block_size), lambda j: (0, at + j))
    in_specs = [
        pl.BlockSpec((1, block_size, cells), lambda j: (j, 0, 0)),
        columns,
        columns,
        pl.BlockSpec((1, block_size, block_size), lambda j: (at + j, 0, 0)),
    ]
    operands = [permuted, cotangent, hidden, w_second]
    aliases = {}
    if denoised is not None:
        in_specs.append(pl.BlockSpec(memory_space=pl.ANY))
        operands.append(denoised)
        aliases = {4: 0}
    return pl.pallas_call(
        second_body,
        grid=(step,),
        in_specs=in_specs,
        out_specs=[columns, pl.BlockSpec((1, block_size, block_size), lambda j: (j, 0, 0))],
        out_shape=[
            jax.ShapeDtypeStruct(hidden.shape, jnp.bfloat16),
            jax.ShapeDtypeStruct((step, block_size, block_size), jnp.bfloat16),
        ],
        input_output_aliases=aliases,
        cost_estimate=cost(4 * step * cells * block_size**2, 10 * step * cells * block_size),
    )(*operands)


def on_device(expression, gene_mask, mask_value, w_qkv, w_out, w_first, w_second, cotangent):
    groups = lax.axis_size("gene")
    local_blocks, block_size, _ = w_first.shape
    cell_rows = expression.shape[0]
    width = w_qkv.shape[1] // 3
    pair = block_size // (local_blocks * groups)

    back_chunks = max(min(BACK_CHUNKS, local_blocks // 8), 1)
    back_step = local_blocks // back_chunks
    backs = back_factor(cotangent, w_second, groups, pair, back_chunks)
    backs, expression, gene_mask = lax.optimization_barrier((backs, expression, gene_mask))
    back_recv = [
        lax.all_to_all(back, "gene", split_axis=0, concat_axis=0, tiled=True) for back in backs
    ]

    masked_in = jnp.where(gene_mask == 1, mask_value[None, :], expression)
    masked_late, back_recv[0] = lax.optimization_barrier((masked_in, back_recv[0]))
    query_sum = scattered_projection(masked_late, w_qkv[:, :width], groups, 1)[:, 0]
    pair_sum = scattered_projection(masked_in, w_qkv[:, width:], groups, 2)
    columns = pair_sum.shape[2]
    pieces = jnp.concatenate(
        [normalize(pair_sum[:, 0]), pair_sum[:, 1].astype(jnp.bfloat16)], axis=1
    )
    gathered = lax.all_gather(pieces, "cell", axis=0, tiled=True)
    attended = attend(normalize(query_sum), gathered[:, :columns], gathered[:, columns:])
    if HEADS % groups == 0:
        attended = lax.all_gather(attended, "gene", axis=1, tiled=True)

    first_chunks = max(min(FIRST_CHUNKS, local_blocks * pair // 16), 1)
    first_step = local_blocks // first_chunks
    hidden, *firsts = first_factor(attended, w_out, masked_in, w_first, groups, first_chunks)
    firsts, back_recv = lax.optimization_barrier((firsts, back_recv))
    recv = [
        lax.all_to_all(first, "gene", split_axis=0, concat_axis=0, tiled=True) for first in firsts
    ]

    def share(grad):
        return lax.psum_scatter(
            grad.astype(jnp.bfloat16), "cell", scatter_dimension=1, tiled=True
        ).astype(jnp.float32)

    got = jnp.concatenate([back.transpose(3, 0, 1, 2, 4) for back in back_recv], axis=0)
    got = got.reshape(local_blocks, block_size, cell_rows)
    first_grads = [first_gradient(got, hidden, 0, local_blocks)]
    recv[0], first_grads = lax.optimization_barrier((recv[0], first_grads))
    first_shares = [share(grad) for grad in first_grads]

    denoised, second_shares = None, []
    for index, at in enumerate(range(0, local_blocks, first_step)):
        permuted = (
            recv[index]
            .reshape(groups, local_blocks, first_step, pair, cell_rows)
            .transpose(2, 3, 0, 1, 4)
            .reshape(first_step, block_size, cell_rows)
        )
        denoised, grad_second = second_factor(
            permuted, cotangent, hidden, w_second, at, denoised
        )
        second_shares.append(share(grad_second))
        if index == first_chunks - 3:
            denoised, second_shares = lax.optimization_barrier((denoised, second_shares))
        if index == first_chunks - 2:
            denoised, first_shares = lax.optimization_barrier((denoised, first_shares))
    return (
        denoised,
        jnp.concatenate(first_shares, axis=0),
        jnp.concatenate(second_shares, axis=0),
    )


def solution(mesh):
    placed = (
        P(("grp", "cell"), "gene"),
        P(("grp", "cell"), "gene"),
        P("gene"),
        P("gene", None),
        P(None, "gene"),
        P("gene", None, None),
        P("gene", None, None),
        P(("grp", "cell"), "gene"),
    )
    return jax.shard_map(
        on_device,
        mesh=mesh,
        in_specs=placed,
        out_specs=(
            P(("grp", "cell"), "gene"),
            P(("grp", "gene"), "cell", None),
            P(("grp", "gene"), "cell", None),
        ),
        check_vma=False,
    )
```

time: 688 us -> 603 us (0.88)
  Pallas kernels: 0 us -> 111 us
  matrix products: 138 us -> 51.6 us
  local copies, waits for them, and re-layouts: 128 us -> 43.4 us
  waiting for transfers between devices: 364 us -> 326 us
  starting transfers between devices: 12.4 us -> 29.2 us
    psum x1 -> x0, waiting for transfers between devices: 124 us -> none  [on_device(): lax.psum(qkv_part.astype(jnp.bfloat16), 'gene').astype(jnp.float32)]
    pallas_call x0 -> x5, Pallas kernels: none -> 111 us  [the longest x1 34.1 us: first_factor(): pl.pallas_call(first_body, grid=(local_blocks,), in_specs=[pl.BlockSpec((...]
    dot_general x7 -> x2, matrix products: 103 us -> 37.8 us  [scattered_projection(): jnp.dot(masked_in, weight, preferred_element_type=jnp.float32)]
    reduce_scatter x2 -> x5, waiting for transfers between devices: 15.9 us -> 64.1 us  [the longest x1 33.4 us: scattered_projection(): share = lax.psum_scatter(apart, 'gene', scatter_dimension=0, tiled=False)]
    all_gather x2, waiting for transfers between devices: 30.4 us -> 73.3 us  [the longest x1 57.4 us: on_device(): attended = lax.all_gather(attended, 'gene', axis=1, tiled=True)]
    all_to_all x3 -> x0, local copies, waits for them, and re-layouts: 37 us -> none  [the longest x2 25.3 us: on_device(): lax.all_to_all(back_send, 'gene', split_axis=2, concat_axis=1, tiled=True)]
    all_to_all x2 -> x6, starting transfers between devices: 11.4 us -> 28.8 us  [the longest x4 19 us: on_device(): lax.all_to_all(back, 'gene', split_axis=0, concat_axis=0, tiled=True)]
    unnamed x7 -> x8, local copies, waits for them, and re-layouts: 18 us -> 4.15 us
  transfers between devices with their start and end apart: 7 -> 13, of which waited for: 6 -> 9; matrix products, arithmetic and copies ran while one was open for 33% -> 19% of each run, Pallas kernels for 0% -> 15%
where the time goes in v1:
time: 603 us; the launch traced here: 599 us
  waiting for transfers between devices  326 us (54%)
  Pallas kernels  111 us (18%)
  matrix products  51.6 us (9%)
  local copies, waits for them, and re-layouts  43.4 us (7%)
  starting transfers between devices  29.2 us (5%)
  other arithmetic  24.1 us (4%)
  between operations  14.3 us (2%)
    all_to_all x2, waiting for transfers between devices, on_device(): lax.all_to_all(first, 'gene', split_axis=0, concat_axis=0, tiled=True)  123 us
    all_to_all x4, waiting for transfers between devices, on_device(): lax.all_to_all(back, 'gene', split_axis=0, concat_axis=0, tiled=True)  65.3 us
    all_gather x1, waiting for transfers between devices, on_device(): attended = lax.all_gather(attended, 'gene', axis=1, tiled=True)  57.4 us
    dot_general x2, matrix products, scattered_projection(): jnp.dot(masked_in, weight, preferred_element_type=jnp.float32)  37.8 us
    pallas_call x1, Pallas kernels, first_factor(): pl.pallas_call(first_body, grid=(local_blocks,), in_specs=[pl.BlockSpec((...  34.1 us
    reduce_scatter x1, waiting for transfers between devices, scattered_projection(): share = lax.psum_scatter(apart, 'gene', scatter_dimension=0, tiled=False)  33.4 us
    reduce_scatter x3, waiting for transfers between devices, share(): lax.psum_scatter(grad.astype(jnp.bfloat16), 'cell', scatter_dimension=1,...  30.7 us
    pallas_call x2, Pallas kernels, second_factor(): pl.pallas_call(second_body, grid=(step,), in_specs=in_specs, out_specs=[c...  29.3 us
  transfers between devices with their start and end apart: 13, of which 9 were waited for; matrix products, arithmetic and copies ran while one was open for 19% of the time, Pallas kernels for 15%

profile of v1, /device:TPU:0, one launch (start us, length us, event | category | flops | bytes accessed | tf_op | source)
XLA Modules:
  0.0 598.8 jit_solution(5827345629248675546)
XLA Ops:
  7.2 23.4 %shard_map.103 = (bf16[4,32,2,8,512]{4,3,2,1,0:T(8,128)(2,1)}, bf16[4,32,2,8,512]{4,3,2,1,0:T(8,128)(2,1)}, bf16[4,32,2,8,512]{4,3,2,1,0:T(8,128)(2,1)}, bf16[4,32,2,8,512]{4,3,2,1,0:T(8,128)(2,1)}) custom-call(bf16[512,8192]{1,0:T(8,128)(2,1)} %cot_ref.5, bf16[32,256,256]{2,1,0:T(8,128)(2,1)} %weight_ref.7), custom_call_target="tpu_custom_call" | custom-call | flops 2147483648 | bytes 20971520 | tf_op jit(solution)/shard_map/pallas_call | solution.py:69
  30.6 6.3 %all-to-all-start = ((bf16[4,32,2,8,512]{4,3,2,1,0:T(8,128)(2,1)}), bf16[4,32,2,8,512]{4,3,2,1,0:T(8,128)(2,1)}, u32[]{:S(2)}, u32[]{:S(2)}) async-start(bf16[4,32,2,8,512]{4,3,2,1,0:T(8,128)(2,1)} %get-tuple-element.38), calls=%async_computation.1 | async-start | bytes 4194304 | tf_op jit(solution)/shard_map/all_to_all | solution.py:202
  36.9 9.0 %compare_select_fusion.masked_ref = bf16[512,8192]{1,0:T(8,128)(2,1)S(1)} fusion(bf16[512,8192]{1,0:T(8,128)(2,1)} %param.8, s32[512,8192]{1,0:T(8,128)} %param.9, bf16[8192]{0:T(1024)(128)(2,1)S(1)} %copy-done.3), kind=kLoop, calls=%fused_computation.6 | loop fusion | flops 8388608 | bytes 33570816 | tf_op jit(solution)/shard_map/jit(_where)/select_n | solution.py:205
  49.3 22.2 %fusion.4 = bf16[512,2048]{1,0:T(8,128)(2,1)} fusion(bf16[512,8192]{1,0:T(8,128)(2,1)S(1)} %compare_select_fusion.masked_ref, bf16[8192,3072]{1,0:T(8,128)(2,1)} %param.11), kind=kOutput, calls=%fused_computation.8 | convolution fusion | flops 17180917760 | bytes 44040192 | tf_op jit(solution)/shard_map/dot_general | solution.py:38
  76.5 8.6 %all-to-all-done = bf16[4,32,2,8,512]{4,3,2,1,0:T(8,128)(2,1)} async-done(((bf16[4,32,2,8,512]{4,3,2,1,0:T(8,128)(2,1)}), bf16[4,32,2,8,512]{4,3,2,1,0:T(8,128)(2,1)}, u32[]{:S(2)}, u32[]{:S(2)}) %all-to-all-start) | async-done | bytes 2097184 | tf_op jit(solution)/shard_map/all_to_all | solution.py:202
  85.2 15.7 %fusion.7 = bf16[512,1024]{1,0:T(8,128)(2,1)} fusion(bf16[512,8192]{1,0:T(8,128)(2,1)} %copy-done, bf16[8192,3072]{1,0:T(8,128)(2,1)} %param.11), kind=kOutput, calls=%fused_computation.10 | convolution fusion | flops 8590458880 | bytes 26214400 | tf_op jit(solution)/shard_map/dot_general | solution.py:38
  104.5 33.4 %reduce-scatter.6.cloned.1.call-done = bf16[1,2,512,256]{3,2,1,0:T(8,128)(2,1)} async-done(((bf16[4,2,512,256]{3,2,1,0:T(8,128)(2,1)}), bf16[1,2,512,256]{3,2,1,0:T(8,128)(2,1)}) %reduce-scatter.6.cloned.1.call-update) | async-done | bytes 524304 | tf_op jit(solution)/shard_map/reduce_scatter | solution.py:45
  142.3 40.2 %all-to-all-done.1 = bf16[4,32,2,8,512]{4,3,2,1,0:T(8,128)(2,1)S(1)} async-done(((bf16[4,32,2,8,512]{4,3,2,1,0:T(8,128)(2,1)}), bf16[4,32,2,8,512]{4,3,2,1,0:T(8,128)(2,1)S(1)}, u32[]{:S(2)}, u32[]{:S(2)}) %all-to-all-start.1) | async-done | bytes 2097184 | tf_op jit(solution)/shard_map/all_to_all | solution.py:202
  189.1 15.9 %all-gather.3.cloned.1.call-done = bf16[2048,512]{1,0:T(8,128)(2,1)} async-done(((bf16[512,512]{1,0:T(8,128)(2,1)}), bf16[2048,512]{1,0:T(8,128)(2,1)}) %all-gather.3.cloned.1.call-update) | async-done | bytes 2097168 | tf_op jit(solution)/shard_map/all_gather | solution.py:213
  211.3 7.8 %convert_reduce_fusion = (f32[4,512]{1,0:T(4,128)S(1)}, bf16[4,512,2048]{2,1,0:T(8,128)(2,1)}) fusion(bf16[2048,4,64]{0,2,1:T(8,128)(2,1)} %bitcast.61, f32[512,4,64]{0,2,1:T(8,128)} %bitcast.54, f32[512,4]{0,1:T(4,128)S(1)} %add_rsqrt_fusion), kind=kOutput, calls=%fused_computation.2 | convolution fusion | flops 553908224 | bytes 9977856 | tf_op jit(solution)/shard_map/qhd,khd->hqk/dot_general | solution.py:27
  219.1 16.5 %all-to-all-done.2 = bf16[4,32,2,8,512]{4,3,2,1,0:T(8,128)(2,1)} async-done(((bf16[4,32,2,8,512]{4,3,2,1,0:T(8,128)(2,1)}), bf16[4,32,2,8,512]{4,3,2,1,0:T(8,128)(2,1)}, u32[]{:S(2)}, u32[]{:S(2)}) %all-to-all-start.2) | async-done | bytes 2097184 | tf_op jit(solution)/shard_map/all_to_all | solution.py:202
  240.1 6.0 %fusion.11 = bf16[512,4,64]{0,2,1:T(8,128)(2,1)S(1)} fusion(bf16[2048,4,64]{0,2,1:T(8,128)(2,1)S(1)} %bitcast.53, bf16[4,512,2048]{2,1,0:T(8,128)(2,1)} %get-tuple-element.64, f32[512,4]{0,1:T(4,128)S(1)} %bitcast.62), kind=kOutput, calls=%fused_computation.13 | convolution fusion | flops 537133056 | bytes 9707520 | tf_op jit(solution)/shard_map/hqk,khd->qhd/dot_general | solution.py:32
  247.0 57.4 %all-gather.5.cloned.1.call-done.attended_ref = bf16[512,1024]{1,0:T(8,128)(2,1)} async-done(((bf16[512,256]{1,0:T(8,128)(2,1)}), bf16[512,1024]{1,0:T(8,128)(2,1)}) %all-gather.5.cloned.1.call-update) | async-done | bytes 1048592 | tf_op jit(solution)/shard_map/all_gather | solution.py:216
  304.4 34.1 %shard_map.104 = (bf16[512,8192]{1,0:T(8,128)(2,1)}, bf16[4,32,32,512]{3,2,1,0:T(8,128)(2,1)}, bf16[4,32,32,512]{3,2,1,0:T(8,128)(2,1)}) custom-call(bf16[512,1024]{1,0:T(8,128)(2,1)} %all-gather.5.cloned.1.call-done.attended_ref, bf16[1024,8192]{1,0:T(8,128)(2,1)} %out_weight_ref.1, bf16[512,8192]{1,0:T(8,128)(2,1)} %copy-done, bf16[32,256,256]{2,1,0:T(8,128)(2,1)} %weight_ref.5), custom_call_target="tpu_custom_call" | custom-call | flops 10737418240 | bytes 46137344 | tf_op jit(solution)/shard_map/pallas_call | solution.py:109
  343.7 6.7 %pad_maximum_fusion = bf16[32,4,32,2,512]{4,0,3,2,1:T(8,128)(2,1)} fusion(bf16[8,4,32,2,512]{4,0,3,2,1:T(8,128)(2,1)} %bitcast.20, bf16[8,4,32,2,512]{4,0,3,2,1:T(8,128)(2,1)} %bitcast.19, bf16[8,4,32,2,512]{4,0,3,2,1:T(8,128)(2,1)S(1)} %bitcast.52, bf16[8,4,32,2,512]{4,0,3,2,1:T(8,128)(2,1)} %bitcast.17), kind=kLoop, calls=%fused_computation.7 | loop fusion | flops 33554432 | bytes 16777216 | tf_op jit(solution)/shard_map/concatenate | solution.py:231
  350.4 11.4 %copy.32.got_ref = bf16[32,256,512]{2,1,0:T(8,128)(2,1)} copy(bf16[32,256,512]{2,0,1:T(8,128)(2,1)} %bitcast.48) | data formatting | bytes 16777216 | tf_op jit(solution)/shard_map/reshape | solution.py:232
  361.8 23.9 %shard_map.105 = bf16[32,256,256]{2,1,0:T(8,128)(2,1)} custom-call(bf16[32,256,512]{2,1,0:T(8,128)(2,1)} %copy.32.got_ref, bf16[512,8192]{1,0:T(8,128)(2,1)} %get-tuple-element.47.hidden_ref), custom_call_target="tpu_custom_call" | custom-call | flops 2147483648 | bytes 20971520 | tf_op jit(solution)/shard_map/pallas_call | solution.py:136
  385.6 51.5 %all-to-all-done.5 = bf16[4,32,32,512]{3,2,1,0:T(8,128)(2,1)} async-done(((bf16[4,32,32,512]{3,2,1,0:T(8,128)(2,1)}), bf16[4,32,32,512]{3,2,1,0:T(8,128)(2,1)}, u32[]{:S(2)}, u32[]{:S(2)}) %all-to-all-start.5) | async-done | bytes 4194336 | tf_op jit(solution)/shard_map/all_to_all | solution.py:223
  442.0 6.6 %copy.33 = bf16[4,32,32,512]{3,1,0,2:T(8,128)(2,1)} copy(bf16[4,32,32,512]{3,2,1,0:T(8,128)(2,1)} %all-to-all-done.5) | data formatting | bytes 8388608 | tf_op jit(solution)/shard_map/reshape | solution.py:241
  448.7 14.8 %shard_map.106 = (bf16[512,8192]{1,0:T(8,128)(2,1)}, bf16[16,256,256]{2,1,0:T(8,128)(2,1)}) custom-call(bf16[16,256,512]{2,1,0:T(8,128)(2,1)} %bitcast.49, bf16[512,8192]{1,0:T(8,128)(2,1)} %cot_ref.5, bf16[512,8192]{1,0:T(8,128)(2,1)} %get-tuple-element.47.hidden_ref, bf16[32,256,256]{2,1,0:T(8,128)(2,1)} %weight_ref.7), custom_call_target="tpu_custom_call" | custom-call | flops 2147483648 | bytes 20971520 | tf_op jit(solution)/shard_map/pallas_call | solution.py:176
  463.6 71.2 %all-to-all-done.4 = bf16[4,32,32,512]{3,2,1,0:T(8,128)(2,1)} async-done(((bf16[4,32,32,512]{3,2,1,0:T(8,128)(2,1)}), bf16[4,32,32,512]{3,2,1,0:T(8,128)(2,1)}, u32[]{:S(2)}, u32[]{:S(2)}) %all-to-all-start.4) | async-done | bytes 4194336 | tf_op jit(solution)/shard_map/all_to_all | solution.py:223
  534.8 6.5 %copy.31 = bf16[4,32,32,512]{3,1,0,2:T(8,128)(2,1)} copy(bf16[4,32,32,512]{3,2,1,0:T(8,128)(2,1)} %all-to-all-done.4) | data formatting | bytes 8388608 | tf_op jit(solution)/shard_map/reshape | solution.py:241
  544.1 14.5 %shard_map.107 = (bf16[512,8192]{1,0:T(8,128)(2,1)}, bf16[16,256,256]{2,1,0:T(8,128)(2,1)}) custom-call(bf16[16,256,512]{2,1,0:T(8,128)(2,1)} %bitcast.50, bf16[512,8192]{1,0:T(8,128)(2,1)} %cot_ref.5, bf16[512,8192]{1,0:T(8,128)(2,1)} %get-tuple-element.47.hidden_ref, bf16[32,256,256]{2,1,0:T(8,128)(2,1)} %weight_ref.7, ...), custom_call_target="tpu_custom_call", output_to_operand_aliasing={{0}: (4, {})} | custom-call | flops 2147483648 | bytes 20971520 | tf_op jit(solution)/shard_map/pallas_call | solution.py:176
  558.7 30.7 %reduce-scatter.14.cloned.1.call-done = bf16[16,64,256]{2,1,0:T(8,128)(2,1)} async-done(((bf16[16,256,256]{2,1,0:T(8,128)(2,1)}), bf16[16,64,256]{2,1,0:T(8,128)(2,1)}) %reduce-scatter.14.cloned.1.call-update) | async-done | bytes 524304 | tf_op jit(solution)/shard_map/reduce_scatter | solution.py:227
  (51 shorter events, 50.4 us)
Async XLA Ops:
  7.2 29.7 %copy-start.3 = (bf16[8192]{0:T(1024)(128)(2,1)S(1)}, bf16[8192]{0:T(1024)(128)(2,1)}, u32[]{:S(2)}) copy-start(bf16[8192]{0:T(1024)(128)(2,1)} %param.10) | copy-start | bytes 49156
  30.6 54.6 %all-to-all-start = ((bf16[4,32,2,8,512]{4,3,2,1,0:T(8,128)(2,1)}), bf16[4,32,2,8,512]{4,3,2,1,0:T(8,128)(2,1)}, u32[]{:S(2)}, u32[]{:S(2)}) async-start(bf16[4,32,2,8,512]{4,3,2,1,0:T(8,128)(2,1)} %get-tuple-element.38), calls=%async_computation.1 | async-start | bytes 4194304 | tf_op jit(solution)/shard_map/all_to_all | solution.py:202
  36.9 101.0 %reduce-scatter.6.cloned.1.call-start = ((), (), s32[]{:S(2)}) async-start(), calls=%async_computation.11 | async-start | bytes 2621440 | tf_op jit(solution)/shard_map/reduce_scatter | solution.py:45
  45.9 3.4 copy-start
  76.5 110.7 %reduce-scatter.8.cloned.1.call-start = ((), (), s32[]{:S(2)}) async-start(), calls=%async_computation.13 | async-start | bytes 1310720 | tf_op jit(solution)/shard_map/reduce_scatter | solution.py:42
  100.9 81.6 %all-to-all-start.1 = ((bf16[4,32,2,8,512]{4,3,2,1,0:T(8,128)(2,1)}), bf16[4,32,2,8,512]{4,3,2,1,0:T(8,128)(2,1)S(1)}, u32[]{:S(2)}, u32[]{:S(2)}) async-start(bf16[4,32,2,8,512]{4,3,2,1,0:T(8,128)(2,1)} %get-tuple-element.43), calls=%async_computation.3 | async-start | bytes 4194304 | tf_op jit(solution)/shard_map/all_to_all | solution.py:202
  104.5 100.5 %all-gather.3.cloned.1.call-start = ((), (), s32[]{:S(2)}) async-start(), calls=%async_computation.12 | async-start | bytes 2621440 | tf_op jit(solution)/shard_map/all_gather | solution.py:213
  182.5 53.1 %all-to-all-start.2 = ((bf16[4,32,2,8,512]{4,3,2,1,0:T(8,128)(2,1)}), bf16[4,32,2,8,512]{4,3,2,1,0:T(8,128)(2,1)}, u32[]{:S(2)}, u32[]{:S(2)}) async-start(bf16[4,32,2,8,512]{4,3,2,1,0:T(8,128)(2,1)} %get-tuple-element.44), calls=%async_computation.4 | async-start | bytes 4194304 | tf_op jit(solution)/shard_map/all_to_all | solution.py:202
  188.3 0.8 copy-start.2
  211.3 28.7 %copy-start.1 = (bf16[2048,256]{0,1:T(8,128)(2,1)S(1)}, bf16[2048,256]{0,1:T(8,128)(2,1)}, u32[]{:S(2)}) copy-start(bf16[2048,256]{0,1:T(8,128)(2,1)} %copy.24) | copy-start | bytes 3145732
  235.6 102.9 %all-to-all-start.3 = ((bf16[4,32,2,8,512]{4,3,2,1,0:T(8,128)(2,1)}), bf16[4,32,2,8,512]{4,3,2,1,0:T(8,128)(2,1)}, u32[]{:S(2)}, u32[]{:S(2)}) async-start(bf16[4,32,2,8,512]{4,3,2,1,0:T(8,128)(2,1)} %get-tuple-element.45), calls=%async_computation.5 | async-start | bytes 4194304 | tf_op jit(solution)/shard_map/all_to_all | solution.py:202
  240.0 64.3 %all-gather.5.cloned.1.call-start = ((), (), s32[]{:S(2)}) async-start(), calls=%async_computation.14 | async-start | bytes 1310720 | tf_op jit(solution)/shard_map/all_gather | solution.py:216
  338.5 98.6 %all-to-all-start.5 = ((bf16[4,32,32,512]{3,2,1,0:T(8,128)(2,1)}), bf16[4,32,32,512]{3,2,1,0:T(8,128)(2,1)}, u32[]{:S(2)}, u32[]{:S(2)}) async-start(bf16[4,32,32,512]{3,2,1,0:T(8,128)(2,1)} %get-tuple-element.48), calls=%async_computation.7 | async-start | bytes 8388608 | tf_op jit(solution)/shard_map/all_to_all | solution.py:223
  343.4 197.9 %reduce-scatter.10.cloned.1.call-start = ((), (), s32[]{:S(2)}) async-start(), calls=%async_computation.15 | async-start | bytes 5242880 | tf_op jit(solution)/shard_map/reduce_scatter | solution.py:227
  437.1 97.7 %all-to-all-start.4 = ((bf16[4,32,32,512]{3,2,1,0:T(8,128)(2,1)}), bf16[4,32,32,512]{3,2,1,0:T(8,128)(2,1)}, u32[]{:S(2)}, u32[]{:S(2)}) async-start(bf16[4,32,32,512]{3,2,1,0:T(8,128)(2,1)} %get-tuple-element.46), calls=%async_computation.6 | async-start | bytes 8388608 | tf_op jit(solution)/shard_map/all_to_all | solution.py:223
  442.0 116.7 %reduce-scatter.12.cloned.1.call-start = ((), (), s32[]{:S(2)}) async-start(), calls=%async_computation.16 | async-start | bytes 2621440 | tf_op jit(solution)/shard_map/reduce_scatter | solution.py:227
  463.5 125.8 %reduce-scatter.14.cloned.1.call-start = ((), (), s32[]{:S(2)}) async-start(), calls=%async_computation.17 | async-start | bytes 2621440 | tf_op jit(solution)/shard_map/reduce_scatter | solution.py:227
Sparse Core Ops, SparseCore 0:
  76.6 61.2 reduce-scatter.5
  140.9 38.6 reduce-scatter.7
  181.7 23.2 all-gather.2
  247.1 57.1 all-gather.4
  437.2 43.5 reduce-scatter.9
  484.0 31.3 reduce-scatter.11
  558.8 30.5 reduce-scatter.13
